TPU v7x, 256 devices: a whole 4x4x8 slice. The times are simulated.
256 devices in a mesh: col: 8 (over x, core), row: 32 (over y, z).
Axes of the slice: x: 4, y: 4, z: 8, core: 2. Of those that a mesh axis runs over, the one named last changes fastest.
Arguments:
- features: float32 [32768, 512], P(('row', 'col')), may hold values from -6 to 6
- weight: float32 [512, 512], replicated, may hold values from -0.25 to 0.25
- tiles: bfloat16 [8, 32, 48, 128, 128], P('col', 'row'), may hold values from -0.09375 to 0.09375
- tile_rows: int32 [8, 32, 48], P('col', 'row'), may hold values from 0 to 31, as said below
- tile_cols: int32 [8, 32, 48], P('col', 'row'), may hold values from 0 to 7
- tile_count: int32 [8, 32], P('col', 'row'), may hold values from 1 to 48, as said below
- cotangent: bfloat16 [32768, 512], P(('col', 'row')), may hold values from -6 to 6
Outputs:
- aggregated: bfloat16 [32768, 512], P(('col', 'row'))
- grad_x: float32 [32768, 512], P(('row', 'col'))
- grad_w: float32 [512, 512], replicated
Inputs may be any that keep to these rules, and one draw needn't show every extreme that they name: `tile_rows`: within one grid block the live slots name distinct tiles. `tile_count`: some grid block has all 48 slots live.
All inputs are finite; a program needn't handle non-finite values.
Results may differ from a plain program's by a relative error of at most 0.0049.
Values may be sent and summed in bfloat16 or wider, within the bound.
No kernel may reach another device: no remote copies, remote signals or barrier semaphores. Data moves between devices by JAX's collectives and lax.ppermute only.
A program may use at most 128 MiB of HBM per device.

v0:
```python
import jax
import jax.numpy as jnp
from jax import lax
from jax.sharding import PartitionSpec as P


def shards(features, weight, tiles, tile_rows, tile_cols, tile_count, cotangent):
    tile_size = tiles.shape[-1]
    slot_count = tiles.shape[2]
    feat_width = features.shape[1]
    blocks = tiles[0, 0]
    rows_idx = tile_rows[0, 0]
    cols_idx = tile_cols[0, 0]
    live_slots = jnp.arange(slot_count, dtype=jnp.int32) < tile_count[0, 0]
    local_rows = jnp.dot(
        features, weight, precision=lax.Precision.HIGHEST, preferred_element_type=jnp.float32
    ).astype(jnp.bfloat16)
    source = lax.all_gather(local_rows, "col", axis=0, tiled=True)
    source_tiles = source.reshape(-1, tile_size, feat_width)
    src_count = source_tiles.shape[0]
    out_tiles = lax.axis_size("row") * features.shape[0] // tile_size
    picked = jnp.take(source_tiles, cols_idx, axis=0)
    tile_terms = jnp.einsum("tab,tbf->taf", blocks, picked, preferred_element_type=jnp.float32)
    select_dst = (
        (rows_idx[None, :] == jnp.arange(out_tiles, dtype=jnp.int32)[:, None]) & live_slots[None, :]
    ).astype(jnp.float32)
    partial_value = jnp.einsum(
        "it,taf->iaf", select_dst, tile_terms, precision=lax.Precision.HIGHEST
    )
    partial_value = partial_value.reshape(out_tiles * tile_size, feat_width)
    aggregated = lax.psum_scatter(partial_value, "row", scatter_dimension=0, tiled=True).astype(
        jnp.bfloat16
    )
    gathered = lax.all_gather(cotangent, "row", axis=0, tiled=True)
    grad_tiles = gathered.reshape(out_tiles, tile_size, feat_width)
    picked_grad = jnp.take(grad_tiles, rows_idx, axis=0)
    back_terms = jnp.einsum("tab,taf->tbf", blocks, picked_grad, preferred_element_type=jnp.float32)
    select_src = (
        (cols_idx[None, :] == jnp.arange(src_count, dtype=jnp.int32)[:, None]) & live_slots[None, :]
    ).astype(jnp.float32)
    back_partial = jnp.einsum(
        "kt,tbf->kbf", select_src, back_terms, precision=lax.Precision.HIGHEST
    )
    back_partial = back_partial.reshape(src_count * tile_size, feat_width)
    grad_y = lax.psum_scatter(back_partial, "col", scatter_dimension=0, tiled=True)
    grad_x = jnp.dot(
        grad_y, weight.T, precision=lax.Precision.HIGHEST, preferred_element_type=jnp.float32
    )
    weight_terms = jnp.dot(
        features.T, grad_y, precision=lax.Precision.HIGHEST, preferred_element_type=jnp.float32
    )
    grad_w = lax.psum(weight_terms, ("col", "row"))
    return (aggregated, grad_x, grad_w)


def solution(mesh):
    placed = (
        P(("row", "col"), None),
        P(),
        P("col", "row", None, None, None),
        P("col", "row", None),
        P("col", "row", None),
        P("col", "row"),
        P(("col", "row"), None),
    )
    return jax.shard_map(
        shards,
        mesh=mesh,
        in_specs=placed,
        out_specs=(P(("col", "row"), None), P(("row", "col"), None), P()),
        check_vma=False,
    )
```

profile of v0, /device:TPU:2, one launch (start us, length us, event | category | flops | bytes accessed | tf_op | source)
XLA Modules:
  0.0 670.1 jit_solution(10211312557095690399)
XLA Ops:
  7.2 0.0 all-gather.5.cloned.1.call-start
  7.2 0.7 all-gather.5.cloned.1.call-update
  7.9 0.0 all-gather.3.cloned.1.call-start
  8.0 2.7 convolution_convert_fusion
  10.6 0.0 all-gather.3.cloned.1.call-update
  10.7 0.0 reduce-scatter.5.cloned.1.call-start
  10.7 0.7 fusion.25
  12.1 0.7 compare_and_fusion
  12.7 82.7 %all-gather.5.cloned.1.call-done = bf16[4096,512]{1,0:T(8,128)(2,1)} async-done(((bf16[128,512]{1,0:T(8,128)(2,1)}), bf16[4096,512]{1,0:T(8,128)(2,1)}) %all-gather.5.cloned.1.call-update) | async-done | bytes 4194320 | tf_op jit(solution)/shard_map/all_gather | solution.py:34
  95.4 7.1 %gather_fusion.1 = bf16[48,128,512]{2,1,0:T(8,128)(2,1)} fusion(bf16[32,128,512]{2,1,0:T(8,128)(2,1)} %bitcast.45, s32[1024]{0:T(1024)S(1)} %pad_clamp_fusion), kind=kCustom, calls=%fused_computation.1 | custom fusion | bytes 12583104 | tf_op jit(solution)/shard_map/jit(_take)/gather | solution.py:36
  102.5 9.2 %fusion.4 = f32[48,512,128]{2,1,0:T(8,128)} fusion(bf16[48,128,512]{2,1,0:T(8,128)(2,1)} %gather_fusion.1, pred[48]{0:T(512)(128)(4,1)S(1)} %compare_and_fusion, bf16[1,1,48,128,128]{4,3,2,1,0:T(8,128)(2,1)S(1)} %copy-done), kind=kOutput, calls=%fused_computation.6 | convolution fusion | flops 808452096 | bytes 20447280 | tf_op jit(solution)/shard_map/tab,taf->tbf/dot_general | solution.py:37
  111.7 12.7 %copy.15 = f32[48,512,128]{1,0,2:T(8,128)} copy(f32[48,512,128]{2,1,0:T(8,128)} %fusion.4) | data formatting | bytes 25165824 | tf_op jit(solution)/shard_map/tab,taf->tbf/dot_general | solution.py:37
  124.4 8.2 %fusion = f32[8,128,512]{2,0,1:T(8,128)S(1)} fusion(f32[48,512,128]{1,0,2:T(8,128)} %copy.15, s32[48]{0:T(128)S(1)} %bitcast.47, pred[48]{0:T(512)(128)(4,1)S(1)} %iota_compare_fusion.2), kind=kOutput, calls=%fused_computation.2 | convolution fusion | flops 301990656 | bytes 14680304 | tf_op jit(solution)/shard_map/kt,tbf->kbf/dot_general | solution.py:41
  132.6 2.6 copy.12
  135.2 0.0 reduce-scatter.5.cloned.1.call-update
  135.2 0.2 all-reduce.2.cloned.1.call-start
  135.5 0.0 all-gather.3.cloned.1.call-done
  135.5 6.2 gather_fusion
  141.7 9.4 %fusion.6 = f32[48,512,128]{2,1,0:T(8,128)} fusion(bf16[48,128,512]{2,1,0:T(8,128)(2,1)} %gather_fusion, pred[48]{0:T(512)(128)(4,1)S(1)} %compare_and_fusion.1, bf16[1,1,48,128,128]{4,3,2,1,0:T(8,128)(2,1)S(1)} %copy-done), kind=kOutput, calls=%fused_computation.8 | convolution fusion | flops 808452096 | bytes 20447280 | tf_op jit(solution)/shard_map/tab,tbf->taf/dot_general | solution.py:23
  151.1 12.9 %copy.14 = f32[48,512,128]{1,0,2:T(8,128)} copy(f32[48,512,128]{2,1,0:T(8,128)} %fusion.6) | data formatting | bytes 25165824 | tf_op jit(solution)/shard_map/tab,tbf->taf/dot_general | solution.py:23
  164.0 1.5 reduce-scatter.5.cloned.1.call-done
  165.5 2.9 convolution_bitcast_fusion
  168.4 0.0 reduce-scatter.3.cloned.1.call-start
  168.5 14.4 %fusion.2 = f32[32,128,512]{2,0,1:T(8,128)S(1)} fusion(f32[48,512,128]{1,0,2:T(8,128)} %copy.14, s32[48]{0:T(128)S(1)} %bitcast.48, pred[48]{0:T(512)(128)(4,1)S(1)} %iota_compare_fusion.2), kind=kOutput, calls=%fused_computation.4 | convolution fusion | flops 1207962624 | bytes 20971760 | tf_op jit(solution)/shard_map/it,taf->iaf/dot_general | solution.py:27
  183.0 8.1 %copy.11 = f32[32,128,512]{2,1,0:T(8,128)} copy(f32[32,128,512]{2,0,1:T(8,128)S(1)} %fusion.2) | data formatting | bytes 16777216 | tf_op jit(solution)/shard_map/it,taf->iaf/dot_general | solution.py:27
  191.1 1.2 copy-done.2
  192.3 0.0 copy-done.4
  192.3 1.9 fusion.28
  194.2 235.5 %all-reduce.2.cloned.1.call-done = f32[512,512]{0,1:T(8,128)} async-done(((f32[512,512]{0,1:T(8,128)}), f32[512,512]{0,1:T(8,128)}) %all-reduce.2.cloned.1.call-update) | async-done | bytes 1048592 | tf_op jit(solution)/shard_map/psum | solution.py:52
  429.7 2.5 copy.13
  432.2 229.7 %reduce-scatter.3.cloned.1.call-done = f32[128,512]{1,0:T(8,128)} async-done(((f32[4096,512]{1,0:T(8,128)}), f32[128,512]{1,0:T(8,128)}) %reduce-scatter.3.cloned.1.call-update) | async-done | bytes 262160 | tf_op jit(solution)/shard_map/reduce_scatter | solution.py:31
  661.9 1.6 convert_element_type.9
  (19 shorter events, 0.1 us)
Async XLA Ops:
  7.2 95.3 %copy-start = (bf16[1,1,48,128,128]{4,3,2,1,0:T(8,128)(2,1)S(1)}, bf16[1,1,48,128,128]{4,3,2,1,0:T(8,128)(2,1)}, u32[]{:S(2)}) copy-start(bf16[1,1,48,128,128]{4,3,2,1,0:T(8,128)(2,1)} %param.9) | copy-start | bytes 4718596
  7.2 88.2 %all-gather.5.cloned.1.call-start = ((), (), s32[]{:S(2)}) async-start(), calls=%async_computation.4 | async-start | bytes 4325376 | tf_op jit(solution)/shard_map/all_gather | solution.py:34
  7.9 127.6 %all-gather.3.cloned.1.call-start = ((), (), s32[]{:S(2)}) async-start(), calls=%async_computation.2 | async-start | bytes 1179648 | tf_op jit(solution)/shard_map/all_gather | solution.py:18
  10.7 154.8 %reduce-scatter.5.cloned.1.call-start = ((), (), s32[]{:S(2)}) async-start(), calls=%async_computation.5 | async-start | bytes 2359296 | tf_op jit(solution)/shard_map/reduce_scatter | solution.py:45
  111.7 12.8 %copy-start.5 = (s32[1,1,48]{2,1,0:T(1,128)S(1)}, s32[1,1,48]{2,1,0:T(1,128)}, u32[]{:S(2)}) copy-start(s32[1,1,48]{2,1,0:T(1,128)} %param.11) | copy-start | bytes 580
  135.2 294.5 %all-reduce.2.cloned.1.call-start = ((), (), s32[]{:S(2)}) async-start(), calls=%async_computation.6 | async-start | bytes 2097152 | tf_op jit(solution)/shard_map/psum | solution.py:52
  151.0 14.4 %copy-start.3 = (f32[128,512]{1,0:T(8,128)S(1)}, f32[128,512]{1,0:T(8,128)}, u32[]{:S(2)}) copy-start(f32[128,512]{1,0:T(8,128)} %param.7) | copy-start | bytes 786436
  151.0 17.4 %copy-start.6 = (s32[1,1,48]{2,1,0:T(1,128)S(1)}, s32[1,1,48]{2,1,0:T(1,128)}, u32[]{:S(2)}) copy-start(s32[1,1,48]{2,1,0:T(1,128)} %param.10) | copy-start | bytes 580
  168.4 493.5 %reduce-scatter.3.cloned.1.call-start = ((), (), s32[]{:S(2)}) async-start(), calls=%async_computation.3 | async-start | bytes 8650752 | tf_op jit(solution)/shard_map/reduce_scatter | solution.py:31
  183.0 480.6 %copy-start.1 = (bf16[1,1,48,128,128]{4,3,2,1,0:T(8,128)(2,1)S(1)}, bf16[1,1,48,128,128]{4,3,2,1,0:T(8,128)(2,1)}, u32[]{:S(2)}) copy-start(bf16[1,1,48,128,128]{4,3,2,1,0:T(8,128)(2,1)} %param.9) | copy-start | bytes 4718596
  191.1 1.2 copy-start.2
  191.1 1.3 copy-start.4
Sparse Core Ops, SparseCore 0:
  10.6 84.7 all-gather.4
  97.8 21.4 all-gather.2
  135.3 30.0 reduce-scatter.4
  171.3 258.3 all-reduce.1
  434.1 227.7 reduce-scatter.2
where the time goes:
time: 671 us; the launch traced here: 670 us
  waiting for transfers between devices  550 us (82%)
  local copies, waits for them, and re-layouts  53.4 us (8%)
  matrix products  48.7 us (7%)
  between operations  14.5 us (2%)
    psum x1, waiting for transfers between devices, shards(): grad_w = lax.psum(weight_terms, ('col', 'row'))  235 us
    reduce_scatter x1, waiting for transfers between devices, shards(): lax.psum_scatter(partial_value, 'row', scatter_dimension=0, tiled=True)  230 us
    all_gather x1, waiting for transfers between devices, shards(): gathered = lax.all_gather(cotangent, 'row', axis=0, tiled=True)  82.7 us
    dot_general x1, matrix products, shards(): jnp.einsum('it,taf->iaf', select_dst, tile_terms, precision=lax.Precision...  14.4 us
  transfers between devices with their start and end apart: 5, of which 4 were waited for; matrix products, arithmetic and copies ran while one was open for 15% of the time, Pallas kernels for 0%

commit v1 on v0

--- a/solution.py
+++ b/solution.py
@@ -31,7 +31,9 @@
     aggregated = lax.psum_scatter(partial_value, "row", scatter_dimension=0, tiled=True).astype(
         jnp.bfloat16
     )
-    gathered = lax.all_gather(cotangent, "row", axis=0, tiled=True)
+    gathered = jnp.concatenate(
+        lax.all_to_all(jnp.stack([cotangent] * lax.axis_size("row")), "row", 0, 0), axis=0
+    )
     grad_tiles = gathered.reshape(out_tiles, tile_size, feat_width)
     picked_grad = jnp.take(grad_tiles, rows_idx, axis=0)
     back_terms = jnp.einsum("tab,taf->tbf", blocks, picked_grad, preferred_element_type=jnp.float32)

time: 671 us -> 694 us (1.034)
  starting transfers between devices: 0.38 us -> 12 us
  waiting for transfers between devices: 550 us -> 561 us
    all_to_all x0 -> x1, waiting for transfers between devices: none -> 95 us  [shards(): lax.all_to_all(jnp.stack([cotangent] * lax.axis_size('row')), 'row', 0, 0)]
    all_gather x1 -> x0, waiting for transfers between devices: 82.7 us -> none  [shards(): gathered = lax.all_gather(cotangent, 'row', axis=0, tiled=True)]
    all_to_all x0 -> x1, starting transfers between devices: none -> 11.6 us  [shards(): lax.all_to_all(jnp.stack([cotangent] * lax.axis_size('row')), 'row', 0, 0)]
  transfers between devices with their start and end apart: 5 -> 5, of which waited for: 4 -> 4; matrix products, arithmetic and copies ran while one was open for 15% -> 14% of each run, Pallas kernels for 0% -> 0%
where the time goes in v1:
time: 694 us; the launch traced here: 693 us
  waiting for transfers between devices  561 us (81%)
  local copies, waits for them, and re-layouts  56.5 us (8%)
  matrix products  47.5 us (7%)
  between operations  14.6 us (2%)
  starting transfers between devices  12 us (2%)
    psum x1, waiting for transfers between devices, shards(): grad_w = lax.psum(weight_terms, ('col', 'row'))  236 us
    reduce_scatter x1, waiting for transfers between devices, shards(): lax.psum_scatter(partial_value, 'row', scatter_dimension=0, tiled=True)  230 us
    all_to_all x1, waiting for transfers between devices, shards(): lax.all_to_all(jnp.stack([cotangent] * lax.axis_size('row')), 'row', 0, 0)  95 us
    dot_general x1, matrix products, shards(): jnp.einsum('it,taf->iaf', select_dst, tile_terms, precision=lax.Precision...  14.4 us
  transfers between devices with their start and end apart: 5, of which 4 were waited for; matrix products, arithmetic and copies ran while one was open for 14% of the time, Pallas kernels for 0%

profile of v1, /device:TPU:2, one launch (start us, length us, event | category | flops | bytes accessed | tf_op | source)
XLA Modules:
  0.0 693.4 jit_solution(15520990876580063290)
XLA Ops:
  7.2 0.0 copy-start
  7.2 3.5 stack.2
  10.7 11.6 %all-to-all-start = ((bf16[32,128,512]{2,1,0:T(8,128)(2,1)}), bf16[32,128,512]{2,1,0:T(8,128)(2,1)}, u32[]{:S(2)}, u32[]{:S(2)}) async-start(bf16[32,128,512]{2,1,0:T(8,128)(2,1)} %stack.2), calls=%async_computation.1 | async-start | bytes 8388608 | tf_op jit(solution)/shard_map/all_to_all | solution.py:35
  22.3 0.0 all-gather.2.cloned.1.call-start
  22.4 1.4 convolution_convert_fusion
  23.8 0.0 all-gather.2.cloned.1.call-update
  23.8 0.0 reduce-scatter.5.cloned.1.call-start
  24.5 95.0 %all-to-all-done = bf16[32,128,512]{2,1,0:T(8,128)(2,1)} async-done(((bf16[32,128,512]{2,1,0:T(8,128)(2,1)}), bf16[32,128,512]{2,1,0:T(8,128)(2,1)}, u32[]{:S(2)}, u32[]{:S(2)}) %all-to-all-start) | async-done | bytes 4194336 | tf_op jit(solution)/shard_map/all_to_all | solution.py:35
  119.5 7.1 %gather_fusion.1 = bf16[48,128,512]{2,1,0:T(8,128)(2,1)} fusion(bf16[32,128,512]{2,1,0:T(8,128)(2,1)} %all-to-all-done, s32[1024]{0:T(1024)S(1)} %pad_clamp_fusion), kind=kCustom, calls=%fused_computation.1 | custom fusion | bytes 12583104 | tf_op jit(solution)/shard_map/jit(_take)/gather | solution.py:38
  126.6 9.2 %fusion.4 = f32[48,512,128]{2,1,0:T(8,128)} fusion(bf16[48,128,512]{2,1,0:T(8,128)(2,1)} %gather_fusion.1, pred[48]{0:T(512)(128)(4,1)S(1)} %compare_and_fusion, bf16[1,1,48,128,128]{4,3,2,1,0:T(8,128)(2,1)S(1)} %copy-done), kind=kOutput, calls=%fused_computation.6 | convolution fusion | flops 808452096 | bytes 20447280 | tf_op jit(solution)/shard_map/tab,taf->tbf/dot_general | solution.py:39
  135.8 12.8 %copy.15 = f32[48,512,128]{1,0,2:T(8,128)} copy(f32[48,512,128]{2,1,0:T(8,128)} %fusion.4) | data formatting | bytes 25165824 | tf_op jit(solution)/shard_map/tab,taf->tbf/dot_general | solution.py:39
  148.6 8.2 %fusion = f32[8,128,512]{2,0,1:T(8,128)S(1)} fusion(f32[48,512,128]{1,0,2:T(8,128)} %copy.15, s32[48]{0:T(128)S(1)} %bitcast.45, pred[48]{0:T(512)(128)(4,1)S(1)} %iota_compare_fusion.2), kind=kOutput, calls=%fused_computation.2 | convolution fusion | flops 301990656 | bytes 14680304 | tf_op jit(solution)/shard_map/kt,tbf->kbf/dot_general | solution.py:43
  156.8 2.6 copy.12
  159.4 0.0 reduce-scatter.5.cloned.1.call-update
  159.4 0.2 all-reduce.2.cloned.1.call-start
  159.7 0.0 all-gather.2.cloned.1.call-done
  159.7 6.2 gather_fusion
  165.9 9.4 %fusion.6 = f32[48,512,128]{2,1,0:T(8,128)} fusion(bf16[48,128,512]{2,1,0:T(8,128)(2,1)} %gather_fusion, pred[48]{0:T(512)(128)(4,1)S(1)} %compare_and_fusion.1, bf16[1,1,48,128,128]{4,3,2,1,0:T(8,128)(2,1)S(1)} %copy-done), kind=kOutput, calls=%fused_computation.8 | convolution fusion | flops 808452096 | bytes 20447280 | tf_op jit(solution)/shard_map/tab,tbf->taf/dot_general | solution.py:23
  175.3 12.8 %copy.14 = f32[48,512,128]{1,0,2:T(8,128)} copy(f32[48,512,128]{2,1,0:T(8,128)} %fusion.6) | data formatting | bytes 25165824 | tf_op jit(solution)/shard_map/tab,tbf->taf/dot_general | solution.py:23
  188.1 0.8 reduce-scatter.5.cloned.1.call-done
  188.9 2.9 convolution_bitcast_fusion
  191.8 0.0 all-reduce.2.cloned.1.call-update
  191.8 0.0 reduce-scatter.3.cloned.1.call-start
  191.9 14.4 %fusion.2 = f32[32,128,512]{2,0,1:T(8,128)S(1)} fusion(f32[48,512,128]{1,0,2:T(8,128)} %copy.14, s32[48]{0:T(128)S(1)} %bitcast.46, pred[48]{0:T(512)(128)(4,1)S(1)} %iota_compare_fusion.2), kind=kOutput, calls=%fused_computation.4 | convolution fusion | flops 1207962624 | bytes 20971760 | tf_op jit(solution)/shard_map/it,taf->iaf/dot_general | solution.py:27
  206.3 8.1 %copy.11 = f32[32,128,512]{2,1,0:T(8,128)} copy(f32[32,128,512]{2,0,1:T(8,128)S(1)} %fusion.2) | data formatting | bytes 16777216 | tf_op jit(solution)/shard_map/it,taf->iaf/dot_general | solution.py:27
  214.4 0.0 reduce-scatter.3.cloned.1.call-update
  214.4 0.9 copy-done.4
  215.4 1.9 fusion.28
  217.2 235.7 %all-reduce.2.cloned.1.call-done = f32[512,512]{0,1:T(8,128)} async-done(((f32[512,512]{0,1:T(8,128)}), f32[512,512]{0,1:T(8,128)}) %all-reduce.2.cloned.1.call-update) | async-done | bytes 1048592 | tf_op jit(solution)/shard_map/psum | solution.py:54
  453.0 2.5 copy.13
  455.5 229.8 %reduce-scatter.3.cloned.1.call-done = f32[128,512]{1,0:T(8,128)} async-done(((f32[4096,512]{1,0:T(8,128)}), f32[128,512]{1,0:T(8,128)}) %reduce-scatter.3.cloned.1.call-update) | async-done | bytes 262160 | tf_op jit(solution)/shard_map/reduce_scatter | solution.py:31
  685.3 1.6 convert_element_type.9
  (19 shorter events, 0.1 us)
Async XLA Ops:
  7.2 119.4 %copy-start = (bf16[1,1,48,128,128]{4,3,2,1,0:T(8,128)(2,1)S(1)}, bf16[1,1,48,128,128]{4,3,2,1,0:T(8,128)(2,1)}, u32[]{:S(2)}) copy-start(bf16[1,1,48,128,128]{4,3,2,1,0:T(8,128)(2,1)} %param.9) | copy-start | bytes 4718596
  7.2 15.2 %copy-start.3 = (f32[128,512]{1,0:T(8,128)S(1)}, f32[128,512]{1,0:T(8,128)}, u32[]{:S(2)}) copy-start(f32[128,512]{1,0:T(8,128)} %param.7) | copy-start | bytes 786436
  7.2 15.2 %copy-start.2 = (f32[512,512]{1,0:T(8,128)S(1)}, f32[512,512]{1,0:T(8,128)}, u32[]{:S(2)}) copy-start(f32[512,512]{1,0:T(8,128)} %param.8) | copy-start | bytes 3145732
  7.2 16.6 %copy-start.6 = (s32[1,1,48]{2,1,0:T(1,128)S(1)}, s32[1,1,48]{2,1,0:T(1,128)}, u32[]{:S(2)}) copy-start(s32[1,1,48]{2,1,0:T(1,128)} %param.10) | copy-start | bytes 580
  10.7 108.8 %all-to-all-start = ((bf16[32,128,512]{2,1,0:T(8,128)(2,1)}), bf16[32,128,512]{2,1,0:T(8,128)(2,1)}, u32[]{:S(2)}, u32[]{:S(2)}) async-start(bf16[32,128,512]{2,1,0:T(8,128)(2,1)} %stack.2), calls=%async_computation.1 | async-start | bytes 8388608 | tf_op jit(solution)/shard_map/all_to_all | solution.py:35
  22.3 137.4 %all-gather.2.cloned.1.call-start = ((), (), s32[]{:S(2)}) async-start(), calls=%async_computation.3 | async-start | bytes 1179648 | tf_op jit(solution)/shard_map/all_gather | solution.py:18
  23.8 165.1 %reduce-scatter.5.cloned.1.call-start = ((), (), s32[]{:S(2)}) async-start(), calls=%async_computation.5 | async-start | bytes 2359296 | tf_op jit(solution)/shard_map/reduce_scatter | solution.py:47
  135.8 12.8 %copy-start.5 = (s32[1,1,48]{2,1,0:T(1,128)S(1)}, s32[1,1,48]{2,1,0:T(1,128)}, u32[]{:S(2)}) copy-start(s32[1,1,48]{2,1,0:T(1,128)} %param.11) | copy-start | bytes 580
  159.4 293.6 %all-reduce.2.cloned.1.call-start = ((), (), s32[]{:S(2)}) async-start(), calls=%async_computation.6 | async-start | bytes 2097152 | tf_op jit(solution)/shard_map/psum | solution.py:54
  191.8 493.4 %reduce-scatter.3.cloned.1.call-start = ((), (), s32[]{:S(2)}) async-start(), calls=%async_computation.4 | async-start | bytes 8650752 | tf_op jit(solution)/shard_map/reduce_scatter | solution.py:31
  206.3 480.6 %copy-start.1 = (bf16[1,1,48,128,128]{4,3,2,1,0:T(8,128)(2,1)S(1)}, bf16[1,1,48,128,128]{4,3,2,1,0:T(8,128)(2,1)}, u32[]{:S(2)}) copy-start(bf16[1,1,48,128,128]{4,3,2,1,0:T(8,128)(2,1)} %param.9) | copy-start | bytes 4718596
  214.4 0.9 copy-start.4
Sparse Core Ops, SparseCore 0:
  25.6 25.3 all-gather.1
  159.5 29.2 reduce-scatter.4
  194.9 258.0 all-reduce.1
  457.4 227.8 reduce-scatter.2
